TPU v7x, 512 devices: a whole 4x8x8 slice. The times are simulated.
512 devices in a mesh: dp: 32 (over z, y_lo, core), tensor: 16 (over y_hi, x).
Axes of the slice: x: 4, y: 8 (y_hi: 4, y_lo: 2; y = y_hi * 2 + y_lo), z: 8, core: 2. Of those that a mesh axis runs over, the one named last changes fastest.
Arguments:
- tokens: bfloat16 [8192, 4096], P(('dp', 'tensor')), may hold values from -6 to 6
- norm_gain: float32 [4096], replicated, may hold values from 0.1 to 1.9
- gate_tiles: bfloat16 [16, 32, 16, 4096], P('tensor', 'dp'), may hold values from -0.125 to 0.125
- up_tiles: bfloat16 [16, 32, 16, 4096], P('tensor', 'dp'), may hold values from -0.125 to 0.125
- down_tiles: bfloat16 [16, 32, 16, 4096], P('tensor', 'dp'), may hold values from -0.0625 to 0.0625
- tile_ids: int32 [16, 32, 3, 16], P('tensor', 'dp'), may hold values from 0 to 27, as said below
- tile_counts: int32 [16, 32, 3], P('tensor', 'dp'), may hold values from 8 to 16, as said below
Outputs:
- mixed: bfloat16 [8192, 4096], P(('dp', 'tensor'))
Inputs may be any that keep to these rules, and one draw needn't show every extreme that they name: `tile_ids`: each device's slots of one matrix name distinct tiles of its shard; local tile l lies in tile row l // 14 and tile column l % 14 of the shard. `tile_counts`: only the first count slots of a matrix on a device hold kept tiles; for each matrix some device has all 16 slots kept.
All inputs are finite; a program needn't handle non-finite values.
Results may differ from a plain program's by a relative error of at most 0.014.
Values may be sent and summed in bfloat16 or wider, within the bound.
No kernel may reach another device: no remote copies, remote signals or barrier semaphores. Data moves between devices by JAX's collectives and lax.ppermute only.
A program may use at most 128 MiB of HBM per device.

v0:
```python
import jax
import jax.numpy as jnp
from jax import lax
from jax.sharding import PartitionSpec as P

D = 4096
FF = 14336
TILE = 64


def normalize(values, norm_gain):
    wide = values.astype(jnp.float32)
    meansq = jnp.mean(wide * wide, axis=-1, keepdims=True)
    return (wide * lax.rsqrt(meansq + 1e-05) * norm_gain).astype(jnp.bfloat16)


def unpack_tiles(packed, slot_ids, counts, row_tiles, col_tiles):
    local_tiles = row_tiles * col_tiles
    slots = slot_ids.shape[0]
    active = jnp.arange(slots) < counts
    select = ((slot_ids[:, None] == jnp.arange(local_tiles)[None, :]) & active[:, None]).astype(
        jnp.bfloat16
    )
    placed = jnp.einsum("kl,ke->le", select, packed, preferred_element_type=jnp.float32).astype(
        jnp.bfloat16
    )
    return placed.reshape(row_tiles, col_tiles, TILE, TILE)


def inward_block(packed, slot_ids, counts, row_tiles, col_tiles):
    placed = unpack_tiles(packed, slot_ids, counts, row_tiles, col_tiles)
    return placed.transpose(0, 2, 1, 3).reshape(row_tiles * TILE, col_tiles * TILE)


def outward_block(packed, slot_ids, counts, row_tiles, col_tiles):
    placed = unpack_tiles(packed, slot_ids, counts, row_tiles, col_tiles)
    return placed.transpose(1, 2, 0, 3).reshape(col_tiles * TILE, row_tiles * TILE)


def local(tokens, norm_gain, gate_tiles, up_tiles, down_tiles, tile_ids, tile_counts):
    row_tiles = D // (TILE * lax.axis_size("dp"))
    col_tiles = FF // (TILE * lax.axis_size("tensor"))
    hidden_width = col_tiles * TILE
    group_rows = lax.all_gather(normalize(tokens, norm_gain), "tensor", axis=0, tiled=True)
    empty_rows = jnp.zeros((D, hidden_width), jnp.bfloat16)
    empty_down = jnp.zeros((hidden_width, D), jnp.bfloat16)

    def place_inward(buffers, gate_piece, up_piece, slot_ids, counts, index):
        offset = index * row_tiles * TILE
        gate_block = inward_block(
            gate_piece[index], slot_ids[index, 0], counts[index, 0], row_tiles, col_tiles
        )
        up_block = inward_block(
            up_piece[index], slot_ids[index, 1], counts[index, 1], row_tiles, col_tiles
        )
        gate_buf = lax.dynamic_update_slice(buffers[0], gate_block, (offset, 0))
        up_buf = lax.dynamic_update_slice(buffers[1], up_block, (offset, 0))
        return (gate_buf, up_buf)

    def place_outward(down_buf, down_piece, slot_ids, counts, index):
        offset = index * row_tiles * TILE
        down_block = outward_block(
            down_piece[index], slot_ids[index, 2], counts[index, 2], row_tiles, col_tiles
        )
        return lax.dynamic_update_slice(down_buf, down_block, (0, offset))

    def add_inward(buffers, pieces):
        gate_piece, up_piece, slot_ids, counts = (part[0] for part in pieces)

        def one_peer(index, state):
            return place_inward(state, gate_piece, up_piece, slot_ids, counts, index)

        return lax.fori_loop(0, gate_piece.shape[0], one_peer, buffers)

    gate_buf, up_buf = add_inward(
        (empty_rows, empty_rows),
        (
            lax.all_gather(gate_tiles, "dp", axis=1, tiled=True),
            lax.all_gather(up_tiles, "dp", axis=1, tiled=True),
            lax.all_gather(tile_ids, "dp", axis=1, tiled=True),
            lax.all_gather(tile_counts, "dp", axis=1, tiled=True),
        ),
    )
    gate = jnp.dot(group_rows, gate_buf, preferred_element_type=jnp.float32)
    upward = jnp.dot(group_rows, up_buf, preferred_element_type=jnp.float32)
    hidden = (jax.nn.silu(gate) * upward).astype(jnp.bfloat16)

    def add_outward(down_state, pieces):
        down_piece, slot_ids, counts = (part[0] for part in pieces)

        def one_peer(index, state):
            return place_outward(state, down_piece, slot_ids, counts, index)

        return lax.fori_loop(0, down_piece.shape[0], one_peer, down_state)

    down_buf = add_outward(
        empty_down,
        (
            lax.all_gather(down_tiles, "dp", axis=1, tiled=True),
            lax.all_gather(tile_ids, "dp", axis=1, tiled=True),
            lax.all_gather(tile_counts, "dp", axis=1, tiled=True),
        ),
    )
    partial_value = jnp.dot(hidden, down_buf, preferred_element_type=jnp.float32)
    return lax.psum_scatter(
        partial_value.astype(jnp.bfloat16), "tensor", scatter_dimension=0, tiled=True
    )


def solution(mesh):
    return jax.shard_map(
        local,
        mesh=mesh,
        in_specs=(
            P(("dp", "tensor"), None),
            P(),
            P("tensor", "dp", None, None),
            P("tensor", "dp", None, None),
            P("tensor", "dp", None, None),
            P("tensor", "dp", None, None),
            P("tensor", "dp", None),
        ),
        out_specs=P(("dp", "tensor"), None),
        check_vma=False,
    )
```

profile of v0, /device:TPU:64, one launch (start us, length us, event | category | flops | bytes accessed | tf_op | source)
XLA Modules:
  0.0 671.3 jit_solution(6418779925387759823)
XLA Ops:
  9.8 1.7 fusion.28
  11.6 37.9 %all_gather.21 = s32[1,32,3,16]{3,0,2,1:T(1,128)S(1)} all-gather(s32[1,1,3,16]{3,0,2,1:T(1,128)} %bitcast.73), channel_id=1, replica_groups=mesh['dp'=32,'tensor'=16] {'dp'}, dimensions={1}, use_global_device_ids=true | all-gather | bytes 6336 | tf_op jit(solution)/shard_map/all_gather | solution.py:80
  49.7 30.8 %all_gather.22 = s32[1,32,3]{2,0,1:T(1,128)S(1)} all-gather(s32[1,1,3]{2,0,1:T(1,128)} %bitcast.74), channel_id=1, replica_groups=mesh['dp'=32,'tensor'=16] {'dp'}, dimensions={1}, use_global_device_ids=true | all-gather | bytes 396 | tf_op jit(solution)/shard_map/all_gather | solution.py:81
  80.6 1.4 all-gather.7.cloned.1.call-done
  82.0 71.2 %all-gather.9.cloned.1.call-done = bf16[1,32,16,4096]{3,2,0,1:T(8,128)(2,1)} async-done(((bf16[1,1,16,4096]{3,2,0,1:T(8,128)(2,1)}), bf16[1,32,16,4096]{3,2,0,1:T(8,128)(2,1)}) %all-gather.9.cloned.1.call-update) | async-done | bytes 4194320 | tf_op jit(solution)/shard_map/all_gather | solution.py:79
  153.2 3.8 broadcast_in_dim.24
  157.0 3.9 broadcast_in_dim.24.clone
  161.0 243.7 %while.32 = (s32[]{:T(128)}, bf16[4096,896]{0,1:T(8,128)(2,1)}, bf16[4096,896]{0,1:T(8,128)(2,1)}, s32[32,3,16]{2,1,0:T(4,128)S(1)}, s32[32,3]{0,1:T(4,128)S(1)}...) while((s32[]{:T(128)}, bf16[4096,896]{0,1:T(8,128)(2,1)}, ...), condition=%wide.region_2.0_spmd, body=%wide.region_1.0_spmd.sunk | while | flops 7571238 | bytes 4392575 | solution.py:73
  162.3 1.2 convolution_convert_fusion.7
  165.4 1.2 convolution_convert_fusion.8
  173.0 1.2 convolution_convert_fusion.8
  177.5 1.2 convolution_convert_fusion.7
  185.1 1.3 convolution_convert_fusion.7
  188.2 1.2 convolution_convert_fusion.8
  192.8 1.2 convolution_convert_fusion.7
  200.4 1.2 convolution_convert_fusion.7
  203.5 1.2 convolution_convert_fusion.8
  208.0 1.3 convolution_convert_fusion.7
  211.1 1.3 convolution_convert_fusion.8
  226.3 1.2 convolution_convert_fusion.8
  256.7 1.2 convolution_convert_fusion.8
  279.6 1.2 convolution_convert_fusion.8
  317.7 1.2 convolution_convert_fusion.8
  352.7 1.2 convolution_convert_fusion.7
  404.7 3.9 broadcast_in_dim.25
  408.6 143.1 %while.33 = (s32[]{:T(128)}, bf16[896,4096]{1,0:T(8,128)(2,1)}, s32[32,3,16]{2,1,0:T(4,128)S(1)}, s32[32,3]{0,1:T(4,128)S(1)}, bf16[32,16,4096]{2,1,0:T(8,128)(2...) while((s32[]{:T(128)}, bf16[896,4096]{1,0:T(8,128)(2,1)}, s32[32,3,16]{2,1,0:T(4,128)S(1)}, ...), condition=%wide.region_4.5_spmd, body=%wide.region_3.4_spmd.sunk | while | flops 3785622 | bytes 2196355 | solution.py:94
  450.1 1.2 convolution_convert_fusion.9
  463.5 1.2 convolution_convert_fusion.9
  535.1 1.2 convolution_convert_fusion.9
  551.7 6.2 fusion.30
  558.0 11.4 %convolution_convert_fusion.3 = bf16[256,4096]{1,0:T(8,128)(2,1)} fusion(bf16[896,4096]{1,0:T(8,128)(2,1)} %get-tuple-element.316, bf16[256,4096]{1,0:T(8,128)(2,1)S(1)} %copy-done, bf16[4096,896]{0,1:T(8,128)(2,1)} %get-tuple-element.315, f32[256,896]{1,0:T(8,128)S(1)} %fusion.30), kind=kOutput, calls=%fused_computation.39 | convolution fusion | flops 3760521216 | bytes 19791872 | tf_op jit(solution)/shard_map/dot_general | solution.py:104
  569.4 95.4 %reduce-scatter.2.cloned.1.call-done = bf16[16,4096]{1,0:T(8,128)(2,1)} async-done(((bf16[256,4096]{1,0:T(8,128)(2,1)}), bf16[16,4096]{1,0:T(8,128)(2,1)}) %reduce-scatter.2.cloned.1.call-update) | async-done | bytes 131088 | tf_op jit(solution)/shard_map/reduce_scatter | solution.py:105
  (672 shorter events, 362.7 us)
Async XLA Ops:
  6.5 75.5 %all-gather.7.cloned.1.call-start = ((), (), s32[]{:S(2)}) async-start(), calls=%async_computation.2 | async-start | bytes 4325376 | tf_op jit(solution)/shard_map/all_gather | solution.py:78
  7.3 145.9 %all-gather.9.cloned.1.call-start = ((), (), s32[]{:S(2)}) async-start(), calls=%async_computation.3 | async-start | bytes 4325376 | tf_op jit(solution)/shard_map/all_gather | solution.py:79
  8.0 396.7 %all-gather.11.cloned.1.call-start = ((), (), s32[]{:S(2)}) async-start(), calls=%async_computation.4 | async-start | bytes 4325376 | tf_op jit(solution)/shard_map/all_gather | solution.py:99
  8.7 543.0 %all-gather.5.cloned.1.call-start = ((), (), s32[]{:S(2)}) async-start(), calls=%async_computation.1 | async-start | bytes 2228224 | tf_op jit(solution)/shard_map/all_gather | solution.py:44
  11.5 653.2 %reduce-scatter.2.cloned.1.call-start = ((), (), s32[]{:S(2)}) async-start(), calls=%async_computation.5 | async-start | bytes 2228224 | tf_op jit(solution)/shard_map/reduce_scatter | solution.py:105
  551.7 6.2 copy-start
Sparse Core Ops, SparseCore 0:
  9.5 72.4 all-gather.6
  84.1 69.0 all-gather.8
  155.4 69.4 all-gather.10
  227.7 65.0 all-gather.4
  569.5 95.2 reduce-scatter.1
where the time goes:
time: 676 us; the launch traced here: 671 us
  local copies, waits for them, and re-layouts  213 us (32%)
  waiting for transfers between devices  170 us (25%)
  matrix products  137 us (20%)
  blocking collectives  68.7 us (10%)
  other arithmetic  64.8 us (10%)
  between operations  13.2 us (2%)
    dot_general x96, matrix products, unpack_tiles(): jnp.einsum('kl,ke->le', select, packed, preferred_element_type=jnp.float32)  119 us
    reduce_scatter x1, waiting for transfers between devices, local(): lax.psum_scatter(partial_value.astype(jnp.bfloat16), 'tensor', scatter_di...  95.4 us
    all_gather x1, waiting for transfers between devices, local(): lax.all_gather(up_tiles, 'dp', axis=1, tiled=True)  71.2 us
    reshape x160, local copies, waits for them, and re-layouts, unpack_tiles(): return placed.reshape(row_tiles, col_tiles, TILE, TILE)  71.1 us
    lt x96, other arithmetic, unpack_tiles(): active = jnp.arange(slots) < counts  62.1 us
    all_gather x1, blocking collectives, local(): lax.all_gather(tile_ids, 'dp', axis=1, tiled=True)  37.9 us
    all_gather x1, blocking collectives, local(): lax.all_gather(tile_counts, 'dp', axis=1, tiled=True)  30.8 us
    dynamic_update_slice x32, local copies, waits for them, and re-layouts, place_inward(): up_buf = lax.dynamic_update_slice(buffers[1], up_block, (offset, 0))  27.4 us
  transfers between devices with their start and end apart: 5, of which 3 were waited for; matrix products, arithmetic and copies ran while one was open for 59% of the time, Pallas kernels for 0%

commit v1 on v0

v1 whole, which is shorter than its diff:
```python
import jax
import jax.numpy as jnp
from jax import lax
from jax.experimental import pallas as pl
from jax.experimental.pallas import tpu as pltpu
from jax.sharding import PartitionSpec as P

D = 4096
FF = 14336
TILE = 64
HALF = TILE // 2
LANES = 2 * TILE
META_ROWS = 16
IN_PEERS = 4
OUT_PEERS = 4


def normalize(values, norm_gain):
    wide = values.astype(jnp.float32)
    meansq = jnp.mean(wide * wide, axis=-1, keepdims=True)
    return (wide * lax.rsqrt(meansq + 1e-05) * norm_gain).astype(jnp.bfloat16)


def slot_table(tile_ids, tile_counts, local_tiles):
    slots = tile_ids.shape[-1]
    order = jnp.arange(slots, dtype=jnp.int32)
    kept = order[None, :] < tile_counts[:, None]
    hit = (tile_ids[:, None, :] == jnp.arange(local_tiles)[None, :, None]) & kept[:, None, :]
    slot = order[None, :] + slots * jnp.arange(3, dtype=jnp.int32)[:, None]
    empty = 3 * slots
    return empty + jnp.sum(jnp.where(hit, slot[:, None, :] - empty, 0), axis=-1)


def feed_forward(table_ref, tokens_ref, gathered_ref, out_ref, tiles_ref, inward_ref, gate_ref, up_ref, hidden_ref, outward_ref, sems, *, peers, slots, row_tiles, col_tiles):
    local_tiles = row_tiles * col_tiles
    body_rows = 3 * slots * HALF
    split = 2 * slots * HALF
    in_chunks = peers // IN_PEERS
    out_chunks = peers // OUT_PEERS
    in_rows = IN_PEERS * row_tiles * TILE

    def inward_copy(chunk):
        where = pl.ds(chunk * IN_PEERS, IN_PEERS)
        return pltpu.make_async_copy(
            gathered_ref.at[where, pl.ds(0, split)], tiles_ref.at[where, pl.ds(0, split)], sems.at[0, chunk]
        )

    def outward_copy(chunk):
        where = pl.ds(chunk * OUT_PEERS, OUT_PEERS)
        rest = pl.ds(split, body_rows - split)
        return pltpu.make_async_copy(gathered_ref.at[where, rest], tiles_ref.at[where, rest], sems.at[1, chunk])

    for chunk in range(in_chunks):
        inward_copy(chunk).start()
    for chunk in range(out_chunks):
        outward_copy(chunk).start()
    tiles_ref[:, body_rows:, :] = jnp.zeros((peers, HALF, LANES), jnp.bfloat16)
    left = lax.broadcasted_iota(jnp.int32, (HALF, LANES), 1) < TILE

    def pair(peer, first, second):
        def load(entry):
            row = pl.multiple_of(table_ref[peer, entry] * HALF, HALF)
            return tiles_ref[peer, pl.ds(row, HALF), :]

        one, two = load(first), load(second)
        even = jnp.where(left, one, pltpu.roll(two, TILE, 1))
        odd = jnp.where(left, pltpu.roll(one, TILE, 1), two)
        return even, odd

    def inward_chunk(chunk, carry):
        inward_copy(chunk).wait()
        for local_peer in range(IN_PEERS):
            peer = chunk * IN_PEERS + local_peer
            for matrix in range(2):
                for row in range(row_tiles):
                    for col in range(0, col_tiles, 2):
                        entry = matrix * local_tiles + row * col_tiles + col
                        even, odd = pair(peer, entry, entry + 1)
                        at = (local_peer * row_tiles + row) * TILE
                        lanes = slice(col * TILE, (col + 2) * TILE)
                        inward_ref[matrix, at : at + HALF, lanes] = even
                        inward_ref[matrix, at + HALF : at + TILE, lanes] = odd
        rows = tokens_ref[:, pl.ds(pl.multiple_of(chunk * in_rows, in_rows), in_rows)]
        gate_ref[...] += jnp.dot(rows, inward_ref[0], preferred_element_type=jnp.float32)
        up_ref[...] += jnp.dot(rows, inward_ref[1], preferred_element_type=jnp.float32)
        return carry

    gate_ref[...] = jnp.zeros_like(gate_ref)
    up_ref[...] = jnp.zeros_like(up_ref)
    lax.fori_loop(0, in_chunks, inward_chunk, 0)

    source = lax.broadcasted_iota(jnp.int32, (LANES, LANES), 0)
    target = lax.broadcasted_iota(jnp.int32, (LANES, LANES), 1)
    inner = target % TILE
    wanted = target - inner + jnp.where(inner < HALF, 2 * inner, 2 * (inner - HALF) + 1)
    shuffle = (source == wanted).astype(jnp.bfloat16)
    for block in range(col_tiles // 2):
        lanes = slice(block * LANES, (block + 1) * LANES)
        value = (jax.nn.silu(gate_ref[:, lanes]) * up_ref[:, lanes]).astype(jnp.bfloat16)
        hidden_ref[:, lanes] = jnp.dot(value, shuffle, preferred_element_type=jnp.float32).astype(jnp.bfloat16)

    out_lanes = OUT_PEERS * LANES

    def outward_chunk(chunk, carry):
        outward_copy(chunk).wait()
        for local_peer in range(OUT_PEERS):
            peer = chunk * OUT_PEERS + local_peer
            for col in range(col_tiles):
                entry = 2 * local_tiles + col
                even, odd = pair(peer, entry, entry + col_tiles)
                lanes = slice(local_peer * LANES, (local_peer + 1) * LANES)
                outward_ref[col * TILE : col * TILE + HALF, lanes] = even
                outward_ref[col * TILE + HALF : (col + 1) * TILE, lanes] = odd
        value = jnp.dot(hidden_ref[...], outward_ref[...], preferred_element_type=jnp.float32)
        out_ref[:, pl.ds(pl.multiple_of(chunk * out_lanes, out_lanes), out_lanes)] = value.astype(jnp.bfloat16)
        return carry

    lax.fori_loop(0, out_chunks, outward_chunk, 0)


def apply_tiles(table, rows, gathered, *, slots, row_tiles, col_tiles, interpret=False):
    import functools

    peers = gathered.shape[0]
    tokens, width = rows.shape
    hidden = col_tiles * TILE
    vmem = pl.BlockSpec(memory_space=pltpu.VMEM)
    return pl.pallas_call(
        functools.partial(feed_forward, peers=peers, slots=slots, row_tiles=row_tiles, col_tiles=col_tiles),
        out_shape=jax.ShapeDtypeStruct((tokens, width), jnp.bfloat16),
        in_specs=[pl.BlockSpec(memory_space=pltpu.SMEM), vmem, pl.BlockSpec(memory_space=pl.ANY)],
        out_specs=vmem,
        scratch_shapes=[
            pltpu.VMEM((peers, 3 * slots * HALF + HALF, LANES), jnp.bfloat16),
            pltpu.VMEM((2, IN_PEERS * row_tiles * TILE, hidden), jnp.bfloat16),
            pltpu.VMEM((tokens, hidden), jnp.float32),
            pltpu.VMEM((tokens, hidden), jnp.float32),
            pltpu.VMEM((tokens, hidden), jnp.bfloat16),
            pltpu.VMEM((hidden, OUT_PEERS * LANES), jnp.bfloat16),
            pltpu.SemaphoreType.DMA((2, max(peers // IN_PEERS, peers // OUT_PEERS))),
        ],
        compiler_params=pltpu.CompilerParams(vmem_limit_bytes=56 * 1024 * 1024),
        interpret=interpret,
        name="feed_forward",
    )(table, rows, gathered)


def pack(gate_tiles, up_tiles, down_tiles, tile_ids, tile_counts, local_tiles):
    tiles = jnp.concatenate([gate_tiles, up_tiles, down_tiles], axis=0)
    tiles = tiles.reshape(tiles.shape[0] * HALF, LANES)
    table = slot_table(tile_ids, tile_counts, local_tiles).astype(jnp.bfloat16)
    meta = jnp.pad(table, ((0, META_ROWS - 3), (0, LANES - local_tiles)))
    return jnp.concatenate([tiles, meta], axis=0)


def even_odd(values):
    rows, width = values.shape
    return values.reshape(rows, width // TILE, HALF, 2).swapaxes(2, 3).reshape(rows, width)


def local(tokens, norm_gain, gate_tiles, up_tiles, down_tiles, tile_ids, tile_counts):
    peers = lax.axis_size("dp")
    members = lax.axis_size("tensor")
    row_tiles = D // (TILE * peers)
    col_tiles = FF // (TILE * members)
    local_tiles = row_tiles * col_tiles
    slots = gate_tiles.shape[2]
    body_rows = 3 * slots * HALF
    packed = pack(gate_tiles[0, 0], up_tiles[0, 0], down_tiles[0, 0], tile_ids[0, 0], tile_counts[0, 0], local_tiles)
    gathered = lax.all_gather(packed, "dp", axis=0)
    mine = even_odd(normalize(tokens, norm_gain))
    copies = jnp.broadcast_to(mine[None], (members,) + mine.shape)
    group_rows = lax.all_to_all(copies, "tensor", 0, 0).reshape(members * mine.shape[0], D)
    table = gathered[:, body_rows : body_rows + 3, :local_tiles].astype(jnp.int32).reshape(peers, 3 * local_tiles)
    partial_value = apply_tiles(
        table, group_rows, gathered, slots=slots, row_tiles=row_tiles, col_tiles=col_tiles
    )
    terms = lax.all_to_all(partial_value.reshape(members, mine.shape[0], D), "tensor", 0, 0)
    return jnp.sum(terms.astype(jnp.float32), axis=0).astype(jnp.bfloat16)


def solution(mesh):
    return jax.shard_map(
        local,
        mesh=mesh,
        in_specs=(
            P(("dp", "tensor"), None),
            P(),
            P("tensor", "dp", None, None),
            P("tensor", "dp", None, None),
            P("tensor", "dp", None, None),
            P("tensor", "dp", None, None),
            P("tensor", "dp", None),
        ),
        out_specs=P(("dp", "tensor"), None),
        check_vma=False,
    )
```

time: 676 us -> 231 us (0.34)
  the two profiles are of different devices: /device:TPU:64 before, /device:TPU:8 now
where the time goes in v1:
time: 231 us; the launch traced here: 230 us
  waiting for transfers between devices  116 us (50%)
  blocking collectives  61.6 us (27%)
  Pallas kernels  19 us (8%)
  between operations  13.5 us (6%)
  starting transfers between devices  8.77 us (4%)
  local copies, waits for them, and re-layouts  6.57 us (3%)
  other arithmetic  4.86 us (2%)
    all_gather x1, waiting for transfers between devices, local(): gathered = lax.all_gather(packed, 'dp', axis=0)  116 us
    all_to_all x1, blocking collectives, local(): lax.all_to_all(partial_value.reshape(members, mine.shape[0], D), 'tensor'...  61.6 us
    pallas_call x1, Pallas kernels, apply_tiles(): pl.pallas_call(functools.partial(feed_forward, peers=peers, slots=slots,...  19 us
    all_to_all x1, starting transfers between devices, local(): lax.all_to_all(copies, 'tensor', 0, 0).reshape(members * mine.shape[0], D)  8.77 us
  transfers between devices with their start and end apart: 2, of which 1 were waited for; matrix products, arithmetic and copies ran while one was open for 2% of the time, Pallas kernels for 0%

profile of v1, /device:TPU:8, one launch (start us, length us, event | category | flops | bytes accessed | tf_op | source)
XLA Modules:
  0.0 230.4 jit_solution(8644729258818155920)
XLA Ops:
  6.5 0.0 copy-start.1
  6.5 0.0 copy-start.2
  6.5 0.0 all-gather.3.cloned.1.call-start
  6.5 0.8 iota_compare_fusion.2
  7.3 0.1 add_add_fusion
  7.4 0.7 copy.14
  8.1 0.1 select_reduce_fusion
  8.2 1.1 pad_maximum_fusion
  9.2 0.2 reshape.72
  9.4 0.8 fusion.1
  10.2 0.0 all-gather.3.cloned.1.call-update
  10.2 0.0 copy-done.1
  10.3 0.1 fusion.2
  10.4 0.0 copy-done.2
  10.4 0.1 fusion.4
  10.5 0.5 copy.10
  11.0 1.1 copy.11
  12.1 0.5 broadcast_in_dim.18
  12.7 1.6 broadcast_in_dim.30
  14.2 8.8 %all-to-all-start = ((bf16[16,16,4096]{2,1,0:T(8,128)(2,1)}), bf16[16,16,4096]{2,1,0:T(8,128)(2,1)S(1)}, u32[]{:S(2)}, u32[]{:S(2)}) async-start(bf16[16,16,4096]{2,1,0:T(8,128)(2,1)} %broadcast_in_dim.30), calls=%async_computation | async-start | bytes 4194304 | tf_op jit(solution)/shard_map/all_to_all | solution.py:173
  23.0 116.1 %all-gather.3.cloned.1.call-done = bf16[49664,128]{1,0:T(8,128)(2,1)} async-done(((bf16[1552,128]{1,0:T(8,128)(2,1)}), bf16[49664,128]{1,0:T(8,128)(2,1)}) %all-gather.3.cloned.1.call-update) | async-done | bytes 12714000 | tf_op jit(solution)/shard_map/all_gather | solution.py:170
  139.1 0.9 slice_convert_fusion
  140.0 0.7 reshape.79.table_ref
  140.7 0.0 all-to-all-done
  140.7 0.0 copy-start
  140.7 1.3 copy-done
  142.0 19.0 %feed_forward.1 = bf16[256,4096]{1,0:T(8,128)(2,1)} custom-call(s32[32,84]{1,0:T(8,128)} %reshape.79.table_ref, bf16[256,4096]{1,0:T(8,128)(2,1)} %bitcast.15, bf16[32,1552,128]{2,1,0:T(8,128)(2,1)} %bitcast.14), custom_call_target="tpu_custom_call" | custom-call | tf_op jit(solution)/shard_map/feed_forward/pallas_call | solution.py:128
  161.0 61.6 %all_to_all.10 = bf16[16,16,4096]{2,1,0:T(8,128)(2,1)S(1)} all-to-all(bf16[16,16,4096]{2,1,0:T(8,128)(2,1)} %bitcast.16), channel_id=1, replica_groups=mesh['dp'=32,'tensor'=16] {'tensor'}, dimensions={0} | all-to-all | bytes 4194304 | tf_op jit(solution)/shard_map/all_to_all | solution.py:178
  222.6 1.0 reduce_sum.32
  (3 shorter events, 0.0 us)
Async XLA Ops:
  6.5 3.7 %copy-start.1 = (bf16[16,4096]{1,0:T(8,128)(2,1)S(1)}, bf16[16,4096]{1,0:T(8,128)(2,1)}, u32[]{:S(2)}) copy-start(bf16[16,4096]{1,0:T(8,128)(2,1)} %param.7) | copy-start | bytes 393220
  6.5 3.9 %copy-start.2 = (f32[4096]{0:T(1024)S(1)}, f32[4096]{0:T(1024)}, u32[]{:S(2)}) copy-start(f32[4096]{0:T(1024)} %param.8) | copy-start | bytes 49156
  6.5 132.6 %all-gather.3.cloned.1.call-start = ((), (), s32[]{:S(2)}) async-start(), calls=%async_computation.2 | async-start | bytes 13111296 | tf_op jit(solution)/shard_map/all_gather | solution.py:170
  14.2 126.5 %all-to-all-start = ((bf16[16,16,4096]{2,1,0:T(8,128)(2,1)}), bf16[16,16,4096]{2,1,0:T(8,128)(2,1)S(1)}, u32[]{:S(2)}, u32[]{:S(2)}) async-start(bf16[16,16,4096]{2,1,0:T(8,128)(2,1)} %broadcast_in_dim.30), calls=%async_computation | async-start | bytes 4194304 | tf_op jit(solution)/shard_map/all_to_all | solution.py:173
  140.7 1.3 copy-start
Sparse Core Ops, SparseCore 0:
  10.4 128.7 all-gather.2

commit v2 on v1

--- a/solution.py
+++ b/solution.py
@@ -59,7 +59,7 @@
 
     def pair(peer, first, second):
         def load(entry):
-            row = pl.multiple_of(table_ref[peer, entry] * HALF, HALF)
+            row = pl.multiple_of(table_ref[peer, entry // local_tiles, entry % local_tiles] * HALF, HALF)
             return tiles_ref[peer, pl.ds(row, HALF), :]
 
         one, two = load(first), load(second)
@@ -158,6 +158,23 @@
     return values.reshape(rows, width // TILE, HALF, 2).swapaxes(2, 3).reshape(rows, width)
 
 
+def group_side(members):
+    side = 1
+    while side * side < members:
+        side *= 2
+    return side
+
+
+def gather_rows(values, groups):
+    copies = jnp.broadcast_to(values[None], (len(groups[0]),) + values.shape)
+    return lax.all_to_all(copies, "tensor", 0, 0, axis_index_groups=groups)
+
+
+def reduce_rows(terms, groups):
+    terms = lax.all_to_all(terms, "tensor", 0, 0, axis_index_groups=groups)
+    return jnp.sum(terms.astype(jnp.float32), axis=0).astype(jnp.bfloat16)
+
+
 def local(tokens, norm_gain, gate_tiles, up_tiles, down_tiles, tile_ids, tile_counts):
     peers = lax.axis_size("dp")
     members = lax.axis_size("tensor")
@@ -169,14 +186,19 @@
     packed = pack(gate_tiles[0, 0], up_tiles[0, 0], down_tiles[0, 0], tile_ids[0, 0], tile_counts[0, 0], local_tiles)
     gathered = lax.all_gather(packed, "dp", axis=0)
     mine = even_odd(normalize(tokens, norm_gain))
-    copies = jnp.broadcast_to(mine[None], (members,) + mine.shape)
-    group_rows = lax.all_to_all(copies, "tensor", 0, 0).reshape(members * mine.shape[0], D)
-    table = gathered[:, body_rows : body_rows + 3, :local_tiles].astype(jnp.int32).reshape(peers, 3 * local_tiles)
+    rows = mine.shape[0]
+    across = group_side(members)
+    along = members // across
+    x_groups = [[y * across + x for x in range(across)] for y in range(along)]
+    y_groups = [[y * across + x for y in range(along)] for x in range(across)]
+    group_rows = gather_rows(mine, y_groups)
+    group_rows = gather_rows(group_rows.reshape(along * rows, D), x_groups).reshape(members * rows, D)
+    table = gathered[:, body_rows : body_rows + 3, :local_tiles].astype(jnp.int32)
     partial_value = apply_tiles(
         table, group_rows, gathered, slots=slots, row_tiles=row_tiles, col_tiles=col_tiles
     )
-    terms = lax.all_to_all(partial_value.reshape(members, mine.shape[0], D), "tensor", 0, 0)
-    return jnp.sum(terms.astype(jnp.float32), axis=0).astype(jnp.bfloat16)
+    summed = reduce_rows(partial_value.reshape(across, along * rows, D), x_groups)
+    return reduce_rows(summed.reshape(along, rows, D), y_groups)
 
 
 def solution(mesh):

time: 231 us -> 184 us (0.80)
  the two profiles are of different devices: /device:TPU:8 before, /device:TPU:64 now
where the time goes in v2:
time: 184 us
  blocking collectives  76.4 us (42%)
  waiting for transfers between devices  59.3 us (32%)
  Pallas kernels  19 us (10%)
  between operations  13.5 us (7%)
  local copies, waits for them, and re-layouts  5.91 us (3%)
  other arithmetic  5.66 us (3%)
  starting transfers between devices  4.29 us (2%)
    all_gather x1, waiting for transfers between devices, local(): gathered = lax.all_gather(packed, 'dp', axis=0)  59.3 us
    all_to_all x2, blocking collectives, reduce_rows(): terms = lax.all_to_all(terms, 'tensor', 0, 0, axis_index_groups=groups)  53.2 us
    all_to_all x1, blocking collectives, gather_rows(): return lax.all_to_all(copies, 'tensor', 0, 0, axis_index_groups=groups)  23.2 us
    pallas_call x1, Pallas kernels, apply_tiles(): pl.pallas_call(functools.partial(feed_forward, peers=peers, slots=slots,...  19 us
    all_to_all x1, starting transfers between devices, gather_rows(): return lax.all_to_all(copies, 'tensor', 0, 0, axis_index_groups=groups)  4.29 us
  transfers between devices with their start and end apart: 2, of which 1 were waited for; matrix products, arithmetic and copies ran while one was open for 3% of the time, Pallas kernels for 0%

profile of v2, /device:TPU:64, one launch (start us, length us, event | category | flops | bytes accessed | tf_op | source)
XLA Modules:
  0.0 184.0 jit_solution(17045710974902627942)
XLA Ops:
  6.5 0.0 copy-start.1
  6.5 0.0 copy-start.2
  6.5 0.0 all-gather.3.cloned.1.call-start
  6.5 0.8 iota_compare_fusion.2
  7.3 0.1 add_add_fusion
  7.4 0.7 copy.14
  8.1 0.1 select_reduce_fusion
  8.2 1.1 pad_maximum_fusion
  9.2 0.2 reshape.71
  9.4 0.8 fusion.1
  10.2 0.0 all-gather.3.cloned.1.call-update
  10.2 0.0 copy-done.1
  10.3 0.1 fusion.2
  10.4 0.0 copy-done.2
  10.4 0.1 fusion.4
  10.5 0.5 copy.10
  11.0 1.1 copy.11
  12.1 0.5 broadcast_in_dim.36
  12.7 23.2 %all_to_all.20 = bf16[4,16,4096]{2,1,0:T(8,128)(2,1)S(1)} all-to-all(bf16[4,16,4096]{2,1,0:T(8,128)(2,1)S(1)} %broadcast_in_dim.37), channel_id=1, replica_groups={{0,4,8,12},{1,5,9,13},{2,6,10,14},{3,7,11,15},{16,20,24,28},{17,21,25,2..., dimensions={0} | all-to-all | bytes 1048576 | tf_op jit(solution)/shard_map/all_to_all | solution.py:170
  35.9 1.6 broadcast_in_dim.39
  37.5 4.3 %all-to-all-start.1 = ((bf16[4,64,4096]{2,1,0:T(8,128)(2,1)}), bf16[4,64,4096]{2,1,0:T(8,128)(2,1)S(1)}, u32[]{:S(2)}, u32[]{:S(2)}) async-start(bf16[4,64,4096]{2,1,0:T(8,128)(2,1)} %broadcast_in_dim.39), calls=%async_computation.1 | async-start | bytes 4194304 | tf_op jit(solution)/shard_map/all_to_all | solution.py:170
  41.8 59.3 %all-gather.3.cloned.1.call-done = bf16[49664,128]{1,0:T(8,128)(2,1)} async-done(((bf16[1552,128]{1,0:T(8,128)(2,1)}), bf16[49664,128]{1,0:T(8,128)(2,1)}) %all-gather.3.cloned.1.call-update) | async-done | bytes 12714000 | tf_op jit(solution)/shard_map/all_gather | solution.py:187
  101.0 1.5 slice_convert_fusion.table_ref
  102.5 0.0 all-to-all-done.1
  102.5 0.0 copy-start
  102.5 1.3 copy-done
  103.8 19.0 %feed_forward.1 = bf16[256,4096]{1,0:T(8,128)(2,1)} custom-call(s32[32,3,28]{2,1,0:T(4,128)} %slice_convert_fusion.table_ref, bf16[256,4096]{1,0:T(8,128)(2,1)} %bitcast.17, bf16[32,1552,128]{2,1,0:T(8,128)(2,1)} %bitcast.16), custom_call_target="tpu_custom_call" | custom-call | tf_op jit(solution)/shard_map/feed_forward/pallas_call | solution.py:128
  122.8 31.0 %all_to_all.21 = bf16[4,64,4096]{2,1,0:T(8,128)(2,1)S(1)} all-to-all(bf16[4,64,4096]{2,1,0:T(8,128)(2,1)} %bitcast.18), channel_id=1, replica_groups={{0,1,2,3},{4,5,6,7},{8,9,10,11},{12,13,14,15},{16,17,18,19},{20,21,22,2..., dimensions={0} | all-to-all | bytes 4194304 | tf_op jit(solution)/shard_map/all_to_all | solution.py:174
  153.8 0.4 reduce_sum.44
  154.2 22.2 %all_to_all.22 = bf16[4,16,4096]{2,1,0:T(8,128)(2,1)S(1)} all-to-all(bf16[4,16,4096]{2,1,0:T(8,128)(2,1)S(1)} %bitcast.21), channel_id=1, replica_groups={{0,4,8,12},{1,5,9,13},{2,6,10,14},{3,7,11,15},{16,20,24,28},{17,21,25,2..., dimensions={0} | all-to-all | bytes 1048576 | tf_op jit(solution)/shard_map/all_to_all | solution.py:174
  176.4 0.7 reduce_sum.45
  (4 shorter events, 0.1 us)
Async XLA Ops:
  6.5 3.7 %copy-start.1 = (bf16[16,4096]{1,0:T(8,128)(2,1)S(1)}, bf16[16,4096]{1,0:T(8,128)(2,1)}, u32[]{:S(2)}) copy-start(bf16[16,4096]{1,0:T(8,128)(2,1)} %param.7) | copy-start | bytes 393220
  6.5 3.9 %copy-start.2 = (f32[4096]{0:T(1024)S(1)}, f32[4096]{0:T(1024)}, u32[]{:S(2)}) copy-start(f32[4096]{0:T(1024)} %param.8) | copy-start | bytes 49156
  6.5 94.5 %all-gather.3.cloned.1.call-start = ((), (), s32[]{:S(2)}) async-start(), calls=%async_computation.4 | async-start | bytes 13111296 | tf_op jit(solution)/shard_map/all_gather | solution.py:187
  37.5 65.0 %all-to-all-start.1 = ((bf16[4,64,4096]{2,1,0:T(8,128)(2,1)}), bf16[4,64,4096]{2,1,0:T(8,128)(2,1)S(1)}, u32[]{:S(2)}, u32[]{:S(2)}) async-start(bf16[4,64,4096]{2,1,0:T(8,128)(2,1)} %broadcast_in_dim.39), calls=%async_computation.1 | async-start | bytes 4194304 | tf_op jit(solution)/shard_map/all_to_all | solution.py:170
  102.5 1.3 copy-start
Sparse Core Ops, SparseCore 0:
  10.4 90.6 all-gather.2
